TPU v7x, 256 devices: a whole 4x4x8 slice. The times are simulated.
256 devices in a mesh: seq: 64 (over z, x, core), tp: 4 (over y).
Axes of the slice: x: 4, y: 4, z: 8, core: 2. Of those that a mesh axis runs over, the one named last changes fastest.
Arguments:
- hidden: bfloat16 [32768, 4096], P(('seq', 'tp')), may hold values from -640 to 640
- norm_gain: float32 [4096], replicated, may hold values from 0.5 to 1.5
- w_query: bfloat16 [4096, 2048], P(None, 'tp'), may hold values from -0.078125 to 0.078125
- w_key: bfloat16 [4096, 1024], P(None, 'tp'), may hold values from -2.421875 to 2.421875
- w_value: bfloat16 [4096, 1024], P(None, 'tp'), may hold values from -0.09375 to 0.09375
- doc_start: int32 [32768], P('seq'), may hold values from 0 to 32767, as said below
- block_owner: int32 [1024], P('seq'), may hold values from 0 to 63, as said below
Outputs:
- context_rows: bfloat16 [32768, 2048], P(('seq', 'tp'))
- key_cache: bfloat16 [49152, 1024], P('seq', 'tp')
- value_cache: bfloat16 [49152, 1024], P('seq', 'tp')
Inputs may be any that keep to these rules, and one draw needn't show every extreme that they name: `doc_start`: rows with equal values form one document: consecutive rows beginning at the row whose number is that value. Every document has at most 256 rows and one has exactly 256; all but the last have at least 64. `block_owner`: owner numbers never fall along the blocks. Owner o holds the blocks from o * 16 + e(o) up to (o + 1) * 16 + e(o + 1) - 1, where -4 <= e <= 4 and e is 0 at both ends of the axis; so an owner holds between 8 and 24 blocks, and some owner holds exactly 24.
All inputs are finite; a program needn't handle non-finite values.
Results may differ from a plain program's by a relative error of at most 0.0078.
Values may be sent and summed in bfloat16 or wider, within the bound.
No kernel may reach another device: no remote copies, remote signals or barrier semaphores. Data moves between devices by JAX's collectives and lax.ppermute only.
A program may use at most 128 MiB of HBM per device.

v0:
```python
import jax
import jax.numpy as jnp
from jax import lax
from jax.sharding import PartitionSpec as P

HD = 128
DOC_MAX = 256
EPS = 1e-05
ROPE_BASE = 500000.0


def from_behind(array, axis, by):
    length = lax.axis_size(axis)
    pairs = [(i, i + by) for i in range(length) if 0 <= i + by < length]
    return lax.ppermute(array, axis, pairs)


def rotate(packed, positions, head_count):
    row_count = packed.shape[0]
    head_width = packed.shape[1] // head_count
    half_width = head_width // 2
    frequency = jnp.power(
        ROPE_BASE, -jnp.arange(half_width, dtype=jnp.float32) * (2.0 / head_width)
    )
    angles = positions.astype(jnp.float32)[:, None] * frequency[None, :]
    cosine = jnp.cos(angles)[:, None, :]
    sine_part = jnp.sin(angles)[:, None, :]
    reshaped = packed.reshape(row_count, head_count, head_width)
    first_half = reshaped[:, :, :half_width]
    second = reshaped[:, :, half_width:]
    rotated = jnp.concatenate(
        [first_half * cosine - second * sine_part, second * cosine + first_half * sine_part], axis=2
    )
    return rotated.reshape(row_count, head_count * head_width)


def project(rows_in, norm_gain, w_query, w_key, w_value, positions):
    widened = rows_in.astype(jnp.float32)
    inverse_rms = lax.rsqrt(jnp.mean(widened * widened, axis=1, keepdims=True) + EPS)
    normed = (widened * inverse_rms * norm_gain[None, :]).astype(jnp.bfloat16)
    queries = jnp.dot(normed, w_query, preferred_element_type=jnp.float32)
    keys_f = jnp.dot(normed, w_key, preferred_element_type=jnp.float32)
    values_f = jnp.dot(normed, w_value, preferred_element_type=jnp.float32)
    queries = rotate(queries, positions, queries.shape[1] // HD).astype(jnp.bfloat16)
    keys_f = rotate(keys_f, positions, keys_f.shape[1] // HD).astype(jnp.bfloat16)
    return (queries, keys_f, values_f.astype(jnp.bfloat16))


def attend(
    queries, keys_in, values_in, query_doc, query_row, key_doc, key_row, key_live, offset, reach
):
    row_count = queries.shape[0]
    groups = keys_in.shape[1] // HD
    per_group = queries.shape[1] // keys_in.shape[1]
    window = row_count + reach

    def one_tile(index):
        first = index * row_count
        key_first = first + offset - reach
        near_keys = lax.dynamic_slice_in_dim(keys_in, key_first, window, 0)
        near_values = lax.dynamic_slice_in_dim(values_in, key_first, window, 0)
        near_doc = lax.dynamic_slice_in_dim(key_doc, key_first, window, 0)
        near_row = lax.dynamic_slice_in_dim(key_row, key_first, window, 0)
        near_live = lax.dynamic_slice_in_dim(key_live, key_first, window, 0)
        query_four = queries.reshape(row_count, groups, per_group, HD)
        key_three = near_keys.reshape(window, groups, HD)
        value_three = near_values.reshape(window, groups, HD)
        scores = jnp.einsum(
            "rgjd,kgd->gjrk", query_four, key_three, preferred_element_type=jnp.float32
        ) * HD ** (-0.5)
        allowed = (
            (query_doc[:, None] == near_doc[None, :])
            & (near_row[None, :] <= query_row[:, None])
            & (near_live[None, :] > 0)
        )
        allowed = allowed | (jnp.arange(window)[None, :] == jnp.arange(row_count)[:, None] + reach)
        scores = jnp.where(allowed[None, None], scores, -jnp.inf)
        highest = jnp.max(scores, axis=3, keepdims=True)
        weights = jnp.exp(scores - highest)
        weights = (weights / jnp.sum(weights, axis=3, keepdims=True)).astype(jnp.bfloat16)
        blended = jnp.einsum(
            "gjrk,kgd->rgjd", weights, value_three, preferred_element_type=jnp.float32
        )
        return blended.astype(jnp.bfloat16).reshape(row_count, groups * per_group * HD)

    tiles = lax.map(one_tile, jnp.arange(row_count // row_count, dtype=jnp.int32))
    return tiles.reshape(row_count, queries.shape[1])


def shards(hidden, norm_gain, w_query, w_key, w_value, doc_start, block_owner):
    home_hidden = lax.all_gather(hidden, "tp", axis=0, tiled=True)
    my_index = lax.axis_index("seq")
    home_rows = home_hidden.shape[0]
    home_blocks = block_owner.shape[0]
    block_rows = home_rows // home_blocks
    spill_rows = home_blocks // 4 * block_rows
    frame_size = home_rows + 2 * spill_rows
    all_rows = lax.axis_size("seq") * home_rows
    row_number = my_index * home_rows + jnp.arange(home_rows, dtype=jnp.int32)
    row_owner = jnp.repeat(block_owner, block_rows)
    frame_number = my_index * home_rows - spill_rows + jnp.arange(frame_size, dtype=jnp.int32)
    queries, keys_own, values_own = project(
        home_hidden, norm_gain, w_query, w_key, w_value, row_number - doc_start
    )
    left = from_behind((keys_own, values_own, doc_start), "seq", 1)
    left_live = jnp.ones((home_rows,), jnp.int32) * (my_index > 0).astype(jnp.int32)
    home_context = attend(
        queries,
        jnp.concatenate([left[0], keys_own], axis=0),
        jnp.concatenate([left[1], values_own], axis=0),
        doc_start,
        row_number,
        jnp.concatenate([left[2], doc_start], axis=0),
        jnp.concatenate([row_number - home_rows, row_number], axis=0),
        jnp.concatenate([left_live, jnp.ones((home_rows,), jnp.int32)], axis=0),
        home_rows,
        DOC_MAX,
    )
    arrived = []
    for direction in (1, -1):
        low_row = home_rows - spill_rows if direction == 1 else 0
        payload = (
            keys_own[low_row : low_row + spill_rows],
            values_own[low_row : low_row + spill_rows],
            row_owner[low_row : low_row + spill_rows],
        )
        arrived.append(from_behind((payload[0], payload[1], payload[2]), "seq", direction))
    from_left, from_right = arrived
    frame_keys = jnp.concatenate([from_left[0], keys_own, from_right[0]], axis=0)
    frame_values = jnp.concatenate([from_left[1], values_own, from_right[1]], axis=0)
    frame_owner = jnp.concatenate([from_left[2], row_owner, from_right[2]], axis=0)
    frame_live = (
        (frame_owner == my_index) & (frame_number >= 0) & (frame_number < all_rows)
    ).astype(jnp.int32)
    live_column = frame_live[:, None] > 0
    key_cache = jnp.where(live_column, frame_keys, jnp.zeros((), jnp.bfloat16))
    value_cache = jnp.where(live_column, frame_values, jnp.zeros((), jnp.bfloat16))
    context_rows = lax.all_to_all(home_context, "tp", split_axis=0, concat_axis=1, tiled=True)
    return (context_rows, key_cache, value_cache)


def solution(mesh):
    return jax.shard_map(
        shards,
        mesh=mesh,
        in_specs=(
            P(("seq", "tp"), None),
            P(),
            P(None, "tp"),
            P(None, "tp"),
            P(None, "tp"),
            P("seq"),
            P("seq"),
        ),
        out_specs=(P(("seq", "tp"), None), P("seq", "tp"), P("seq", "tp")),
        check_vma=False,
    )
```

profile of v0, /device:TPU:128, one launch (start us, length us, event | category | flops | bytes accessed | tf_op | source)
XLA Modules:
  0.0 141.9 jit_solution(14735143676403520581)
XLA Ops:
  8.9 3.6 %collective-permute-start.4 = (s32[128]{0:T(128)S(1)}, s32[128]{0:T(128)S(1)}, u32[]{:S(2)}, u32[]{:S(2)}) collective-permute-start(s32[128]{0:T(128)S(1)} %slice.56), channel_id=1, source_target_pairs={{4,0},{8,4},{12,8},{16,12},{20,16},{24,20},{28,24},{32,28},{36,32}... | collective-permute-start | bytes 1544 | tf_op jit(solution)/shard_map/ppermute | solution.py:15
  12.7 1.9 %collective-permute-start.3 = (s32[128]{0:T(128)S(1)}, s32[128]{0:T(128)S(1)}, u32[]{:S(2)}, u32[]{:S(2)}) collective-permute-start(s32[128]{0:T(128)S(1)} %slice.54), channel_id=1, source_target_pairs={{0,4},{4,8},{8,12},{12,16},{16,20},{20,24},{24,28},{28,32},{32,36}... | collective-permute-start | bytes 1544 | tf_op jit(solution)/shard_map/ppermute | solution.py:15
  14.6 1.9 %collective-permute-start.1 = (s32[512]{0:T(512)}, s32[512]{0:T(512)S(1)}, u32[]{:S(2)}, u32[]{:S(2)}) collective-permute-start(s32[512]{0:T(512)} %param.12), channel_id=1, source_target_pairs={{0,4},{4,8},{8,12},{12,16},{16,20},{20,24},{24,28},{28,32},{32,36}... | collective-permute-start | bytes 6152 | tf_op jit(solution)/shard_map/ppermute | solution.py:15
  20.9 2.1 %collective-permute-done.1 = s32[512]{0:T(512)S(1)} collective-permute-done((s32[512]{0:T(512)}, s32[512]{0:T(512)S(1)}, u32[]{:S(2)}, u32[]{:S(2)}) %collective-permute-start.1) | collective-permute-done | bytes 2080 | tf_op jit(solution)/shard_map/ppermute | solution.py:15
  23.8 2.2 %fusion.9 = pred[512,768]{0,1:T(8,128)(4,1)} fusion(s32[512]{0:T(512)S(1)} %iota_add_fusion.1, s32[512]{0:T(512)S(1)} %get-tuple-element.62, s32[512]{0:T(512)} %param.12, s32[768]{0:T(1024)S(1)} %dynamic_slice.25, s32[768]{0:T(1024)S(1)} %dynamic_slice.24, pred[768]{0:T(1024)(128)(4,1)S(1)} %slice_compare_fusion), kind=kLoop, calls=%fused_computation.15 | loop fusion | flops 2359296 | bytes 406272 | tf_op jit(solution)/shard_map/while/body/eval_jaxpr/or | solution.py:76
  25.9 36.2 %all-gather.2.cloned.1.call-done = bf16[512,4096]{1,0:T(8,128)(2,1)} async-done(((bf16[128,4096]{1,0:T(8,128)(2,1)}), bf16[512,4096]{1,0:T(8,128)(2,1)}) %all-gather.2.cloned.1.call-update) | async-done | bytes 4194320 | tf_op jit(solution)/shard_map/all_gather | solution.py:91
  62.1 3.2 %fusion.1 = f32[512]{0:T(512)S(1)} fusion(bf16[512,4096]{1,0:T(8,128)(2,1)} %all-gather.2.cloned.1.call-done), kind=kLoop, calls=%fused_computation.3 | loop fusion | flops 6290944 | bytes 4196352 | tf_op jit(solution)/shard_map/reduce_sum | solution.py:39
  65.6 2.0 %convolution_convert_fusion = bf16[512,256]{1,0:T(8,128)(2,1)} fusion(bf16[4096,256]{1,0:T(8,128)(2,1)S(1)} %copy-done, bf16[512,4096]{1,0:T(8,128)(2,1)S(1)} %copy-done.1, f32[4096]{0:T(1024)S(1)} %copy-done.4, f32[512]{0:T(512)S(1)} %add_rsqrt_fusion), kind=kOutput, calls=%fused_computation.18 | convolution fusion | flops 1082261504 | bytes 6572032 | tf_op jit(solution)/shard_map/dot_general | solution.py:43
  68.5 1.9 %collective-permute-start = (bf16[512,256]{1,0:T(8,128)(2,1)}, bf16[512,256]{1,0:T(8,128)(2,1)}, u32[]{:S(2)}, u32[]{:S(2)}) collective-permute-start(bf16[512,256]{1,0:T(8,128)(2,1)} %convolution_convert_fusion), channel_id=1, source_target_pairs={{0,4},{4,8},{8,12},{12,16},{16,20},{20,24},{24,28},{28,32},{32,36}... | collective-permute-start | bytes 786440 | tf_op jit(solution)/shard_map/ppermute | solution.py:15
  70.5 3.5 %collective-permute-start.7 = (bf16[128,256]{1,0:T(8,128)(2,1)S(1)}, bf16[128,256]{1,0:T(8,128)(2,1)}, u32[]{:S(2)}, u32[]{:S(2)}) collective-permute-start(bf16[128,256]{1,0:T(8,128)(2,1)S(1)} %get-tuple-element.49), channel_id=1, source_target_pairs={{0,4},{4,8},{8,12},{12,16},{16,20},{20,24},{24,28},{28,32},{32,36}... | collective-permute-start | bytes 196616 | tf_op jit(solution)/shard_map/ppermute | solution.py:15
  73.9 5.4 %collective-permute-start.8 = (bf16[128,256]{1,0:T(8,128)(2,1)S(1)}, bf16[128,256]{1,0:T(8,128)(2,1)}, u32[]{:S(2)}, u32[]{:S(2)}) collective-permute-start(bf16[128,256]{1,0:T(8,128)(2,1)S(1)} %get-tuple-element.50), channel_id=1, source_target_pairs={{4,0},{8,4},{12,8},{16,12},{20,16},{24,20},{28,24},{32,28},{36,32}... | collective-permute-start | bytes 196616 | tf_op jit(solution)/shard_map/ppermute | solution.py:15
  79.4 1.6 %fusion.30 = f32[512,256]{0,1:T(8,128)S(1)} fusion(bf16[4096,256]{1,0:T(8,128)(2,1)S(1)} %copy-done.3, bf16[512,4096]{1,0:T(8,128)(2,1)S(1)} %copy-done.1, f32[4096]{0:T(1024)S(1)} %copy-done.4, f32[512]{0:T(512)S(1)} %add_rsqrt_fusion), kind=kOutput, calls=%fused_computation.59 | convolution fusion | flops 1082130432 | bytes 6834176 | tf_op jit(solution)/shard_map/dot_general | solution.py:42
  82.0 1.2 copy.45
  83.2 1.6 %subtract_convert_fusion.1 = (bf16[512,2,64]{2,1,0:T(2,128)(2,1)S(1)}, bf16[512,2,64]{2,1,0:T(2,128)(2,1)S(1)}) fusion(f32[512,2,64]{2,1,0:T(2,128)S(1)} %copy.46, f32[512,2,64]{2,1,0:T(2,128)S(1)} %copy.45, f32[512,64]{1,0:T(8,128)} %copy.32, f32[512,64]{1,0:T(8,128)} %copy.30), kind=kLoop, calls=%fused_computation.24 | loop fusion | flops 524288 | bytes 1048576 | tf_op jit(solution)/shard_map/convert.2
  85.5 1.9 %collective-permute-start.2 = (bf16[512,256]{1,0:T(8,128)(2,1)S(1)}, bf16[512,256]{1,0:T(8,128)(2,1)S(1)}, u32[]{:S(2)}, u32[]{:S(2)}) collective-permute-start(bf16[512,256]{1,0:T(8,128)(2,1)S(1)} %bitcast.51), channel_id=1, source_target_pairs={{0,4},{4,8},{8,12},{12,16},{16,20},{20,24},{24,28},{28,32},{32,36}... | collective-permute-start | bytes 786440 | tf_op jit(solution)/shard_map/ppermute | solution.py:15
  87.4 5.9 %fusion.28 = f32[512,512]{0,1:T(8,128)S(1)} fusion(bf16[4096,512]{1,0:T(8,128)(2,1)} %param.9, bf16[512,4096]{1,0:T(8,128)(2,1)} %all-gather.2.cloned.1.call-done, f32[4096]{0:T(1024)} %param.8, f32[512]{0:T(512)S(1)} %add_rsqrt_fusion), kind=kOutput, calls=%fused_computation.58 | convolution fusion | flops 2155872256 | bytes 9455616 | tf_op jit(solution)/shard_map/dot_general | solution.py:41
  94.0 7.0 %collective-permute-start.6 = (bf16[128,256]{1,0:T(8,128)(2,1)S(1)}, bf16[128,256]{1,0:T(8,128)(2,1)S(1)}, u32[]{:S(2)}, u32[]{:S(2)}) collective-permute-start(bf16[128,256]{1,0:T(8,128)(2,1)S(1)} %bitcast.60), channel_id=1, source_target_pairs={{4,0},{8,4},{12,8},{16,12},{20,16},{24,20},{28,24},{32,28},{36,32}... | collective-permute-start | bytes 196616 | tf_op jit(solution)/shard_map/ppermute | solution.py:15
  100.9 2.1 %collective-permute-start.5 = (bf16[128,256]{1,0:T(8,128)(2,1)S(1)}, bf16[128,256]{1,0:T(8,128)(2,1)S(1)}, u32[]{:S(2)}, u32[]{:S(2)}) collective-permute-start(bf16[128,256]{1,0:T(8,128)(2,1)S(1)} %bitcast.59), channel_id=1, source_target_pairs={{0,4},{4,8},{8,12},{12,16},{16,20},{20,24},{24,28},{28,32},{32,36}... | collective-permute-start | bytes 196616 | tf_op jit(solution)/shard_map/ppermute | solution.py:15
  103.1 6.7 %collective-permute-done.5 = bf16[128,256]{1,0:T(8,128)(2,1)S(1)} collective-permute-done((bf16[128,256]{1,0:T(8,128)(2,1)S(1)}, bf16[128,256]{1,0:T(8,128)(2,1)S(1)}, u32[]{:S(2)}, u32[]{:S(2)}) %collective-permute-start.5) | collective-permute-done | bytes 65568 | tf_op jit(solution)/shard_map/ppermute | solution.py:15
  109.9 2.3 %maximum_select_fusion.1 = (bf16[768,256]{1,0:T(8,128)(2,1)}, bf16[768,256]{1,0:T(8,128)(2,1)S(1)}, bf16[768,256]{1,0:T(8,128)(2,1)S(1)}, bf16[768,256]{1,0:T(8,128)(2,1)}) fusion(bf16[128,256]{1,0:T(8,128)(2,1)} %collective-permute-done.8, bf16[512,256]{1,0:T(8,128)(2,1)} %convolution_convert_fusion, bf16[128,256]{1,0:T(8,128)(2,1)} %collective-permute-done.7, ...), kind=kLoop, calls=%fused_computation.28 | loop fusion | flops 4325376 | bytes 2884352 | tf_op jit(solution)/shard_map/jit(_where)/select_n | solution.py:137
  113.2 6.1 %fusion.36 = (f32[2,2,512]{2,1,0:T(2,128)S(1)}, f32[2,2,512,768]{2,3,1,0:T(8,128)}) fusion(pred[512,768]{0,1:T(8,128)(4,1)} %fusion.9, bf16[512,2,2,128]{0,3,2,1:T(8,128)(2,1)S(1)} %bitcast.53, bf16[768,2,128,1]{2,1,0,3:T(2,128)(2,1)S(1)} %bitcast.56), kind=kOutput, calls=%fused_computation.63 | convolution fusion | flops 408945408 | bytes 7610368 | tf_op jit(solution)/shard_map/while/body/eval_jaxpr/sub | solution.py:79
  119.3 3.4 %fusion.11 = bf16[512,2,2,128]{0,3,2,1:T(8,128)(2,1)S(1)} fusion(bf16[768,2,128,1]{0,2,3,1:T(8,128)(2,1)S(1)} %bitcast.55, f32[2,2,512,768]{2,3,1,0:T(8,128)} %get-tuple-element.60, f32[2,2,512]{2,1,0:T(2,128)S(1)} %get-tuple-element.59), kind=kOutput, calls=%fused_computation.17 | convolution fusion | flops 406061056 | bytes 7217152 | tf_op jit(solution)/shard_map/while/body/eval_jaxpr/gjrk,kgd->rgjd/dot_general | solution.py:81
  122.9 11.2 %all_to_all.19 = bf16[4,128,512]{1,2,0:T(8,128)(2,1)S(1)} all-to-all(bf16[4,128,512]{1,2,0:T(8,128)(2,1)S(1)} %copy.37), channel_id=1, replica_groups=mesh['seq'=64,'tp'=4] {'tp'}, dimensions={0} | all-to-all | bytes 1048576 | tf_op jit(solution)/shard_map/all_to_all | solution.py:138
  134.1 1.0 copy.38
  (55 shorter events, 11.5 us)
Async XLA Ops:
  7.2 58.2 %copy-start = (bf16[4096,256]{1,0:T(8,128)(2,1)S(1)}, bf16[4096,256]{1,0:T(8,128)(2,1)}, u32[]{:S(2)}) copy-start(bf16[4096,256]{1,0:T(8,128)(2,1)} %param.11) | copy-start | bytes 6291460
  7.2 58.2 %copy-start.4 = (f32[4096]{0:T(1024)S(1)}, f32[4096]{0:T(1024)}, u32[]{:S(2)}) copy-start(f32[4096]{0:T(1024)} %param.8) | copy-start | bytes 49156
  7.2 54.9 %all-gather.2.cloned.1.call-start = ((), (), s32[]{:S(2)}) async-start(), calls=%async_computation.1 | async-start | bytes 5242880 | tf_op jit(solution)/shard_map/all_gather | solution.py:91
  8.9 11.4 %collective-permute-start.4 = (s32[128]{0:T(128)S(1)}, s32[128]{0:T(128)S(1)}, u32[]{:S(2)}, u32[]{:S(2)}) collective-permute-start(s32[128]{0:T(128)S(1)} %slice.56), channel_id=1, source_target_pairs={{4,0},{8,4},{12,8},{16,12},{20,16},{24,20},{28,24},{32,28},{36,32}... | collective-permute-start | bytes 1544 | tf_op jit(solution)/shard_map/ppermute | solution.py:15
  12.7 8.2 %collective-permute-start.3 = (s32[128]{0:T(128)S(1)}, s32[128]{0:T(128)S(1)}, u32[]{:S(2)}, u32[]{:S(2)}) collective-permute-start(s32[128]{0:T(128)S(1)} %slice.54), channel_id=1, source_target_pairs={{0,4},{4,8},{8,12},{12,16},{16,20},{20,24},{24,28},{28,32},{32,36}... | collective-permute-start | bytes 1544 | tf_op jit(solution)/shard_map/ppermute | solution.py:15
  14.6 8.4 %collective-permute-start.1 = (s32[512]{0:T(512)}, s32[512]{0:T(512)S(1)}, u32[]{:S(2)}, u32[]{:S(2)}) collective-permute-start(s32[512]{0:T(512)} %param.12), channel_id=1, source_target_pairs={{0,4},{4,8},{8,12},{12,16},{16,20},{20,24},{24,28},{28,32},{32,36}... | collective-permute-start | bytes 6152 | tf_op jit(solution)/shard_map/ppermute | solution.py:15
  62.1 3.4 %copy-start.1 = (bf16[512,4096]{1,0:T(8,128)(2,1)S(1)}, bf16[512,4096]{1,0:T(8,128)(2,1)}, u32[]{:S(2)}) copy-start(bf16[512,4096]{1,0:T(8,128)(2,1)} %all-gather.2.cloned.1.call-done) | copy-start | bytes 12582916
  65.6 13.8 %copy-start.3 = (bf16[4096,256]{1,0:T(8,128)(2,1)S(1)}, bf16[4096,256]{1,0:T(8,128)(2,1)}, u32[]{:S(2)}) copy-start(bf16[4096,256]{1,0:T(8,128)(2,1)} %param.10) | copy-start | bytes 6291460
  68.5 41.3 %collective-permute-start = (bf16[512,256]{1,0:T(8,128)(2,1)}, bf16[512,256]{1,0:T(8,128)(2,1)}, u32[]{:S(2)}, u32[]{:S(2)}) collective-permute-start(bf16[512,256]{1,0:T(8,128)(2,1)} %convolution_convert_fusion), channel_id=1, source_target_pairs={{0,4},{4,8},{8,12},{12,16},{16,20},{20,24},{24,28},{28,32},{32,36}... | collective-permute-start | bytes 786440 | tf_op jit(solution)/shard_map/ppermute | solution.py:15
  70.5 30.5 %collective-permute-start.7 = (bf16[128,256]{1,0:T(8,128)(2,1)S(1)}, bf16[128,256]{1,0:T(8,128)(2,1)}, u32[]{:S(2)}, u32[]{:S(2)}) collective-permute-start(bf16[128,256]{1,0:T(8,128)(2,1)S(1)} %get-tuple-element.49), channel_id=1, source_target_pairs={{0,4},{4,8},{8,12},{12,16},{16,20},{20,24},{24,28},{28,32},{32,36}... | collective-permute-start | bytes 196616 | tf_op jit(solution)/shard_map/ppermute | solution.py:15
  73.9 29.2 %collective-permute-start.8 = (bf16[128,256]{1,0:T(8,128)(2,1)S(1)}, bf16[128,256]{1,0:T(8,128)(2,1)}, u32[]{:S(2)}, u32[]{:S(2)}) collective-permute-start(bf16[128,256]{1,0:T(8,128)(2,1)S(1)} %get-tuple-element.50), channel_id=1, source_target_pairs={{4,0},{8,4},{12,8},{16,12},{20,16},{24,20},{28,24},{32,28},{36,32}... | collective-permute-start | bytes 196616 | tf_op jit(solution)/shard_map/ppermute | solution.py:15
  85.5 24.4 %collective-permute-start.2 = (bf16[512,256]{1,0:T(8,128)(2,1)S(1)}, bf16[512,256]{1,0:T(8,128)(2,1)S(1)}, u32[]{:S(2)}, u32[]{:S(2)}) collective-permute-start(bf16[512,256]{1,0:T(8,128)(2,1)S(1)} %bitcast.51), channel_id=1, source_target_pairs={{0,4},{4,8},{8,12},{12,16},{16,20},{20,24},{24,28},{28,32},{32,36}... | collective-permute-start | bytes 786440 | tf_op jit(solution)/shard_map/ppermute | solution.py:15
  94.0 9.1 %collective-permute-start.6 = (bf16[128,256]{1,0:T(8,128)(2,1)S(1)}, bf16[128,256]{1,0:T(8,128)(2,1)S(1)}, u32[]{:S(2)}, u32[]{:S(2)}) collective-permute-start(bf16[128,256]{1,0:T(8,128)(2,1)S(1)} %bitcast.60), channel_id=1, source_target_pairs={{4,0},{8,4},{12,8},{16,12},{20,16},{24,20},{28,24},{32,28},{36,32}... | collective-permute-start | bytes 196616 | tf_op jit(solution)/shard_map/ppermute | solution.py:15
  100.9 8.9 %collective-permute-start.5 = (bf16[128,256]{1,0:T(8,128)(2,1)S(1)}, bf16[128,256]{1,0:T(8,128)(2,1)S(1)}, u32[]{:S(2)}, u32[]{:S(2)}) collective-permute-start(bf16[128,256]{1,0:T(8,128)(2,1)S(1)} %bitcast.59), channel_id=1, source_target_pairs={{0,4},{4,8},{8,12},{12,16},{16,20},{20,24},{24,28},{28,32},{32,36}... | collective-permute-start | bytes 196616 | tf_op jit(solution)/shard_map/ppermute | solution.py:15
  113.2 6.1 %copy-start.2 = (bf16[768,256]{0,1:T(8,128)(2,1)S(1)}, bf16[768,256]{0,1:T(8,128)(2,1)}, u32[]{:S(2)}) copy-start(bf16[768,256]{0,1:T(8,128)(2,1)} %copy.42) | copy-start | bytes 1179652
Sparse Core Ops, SparseCore 0:
  9.8 52.2 all-gather.1
where the time goes:
time: 143 us; the launch traced here: 142 us
  waiting for transfers between devices  46.3 us (32%)
  starting transfers between devices  29.3 us (20%)
  matrix products  19.1 us (13%)
  between operations  14.4 us (10%)
  other arithmetic  12.5 us (9%)
  blocking collectives  11.2 us (8%)
  local copies, waits for them, and re-layouts  9.14 us (6%)
    all_gather x1, waiting for transfers between devices, shards(): home_hidden = lax.all_gather(hidden, 'tp', axis=0, tiled=True)  36.2 us
    ppermute x9, starting transfers between devices, from_behind(): return lax.ppermute(array, axis, pairs)  29.3 us
    all_to_all x1, blocking collectives, shards(): lax.all_to_all(home_context, 'tp', split_axis=0, concat_axis=1, tiled=True)  11.2 us
    ppermute x9, waiting for transfers between devices, from_behind(): return lax.ppermute(array, axis, pairs)  9.44 us
    sub x1, matrix products, one_tile(): weights = jnp.exp(scores - highest)  6.09 us
    dot_general x1, matrix products, project(): queries = jnp.dot(normed, w_query, preferred_element_type=jnp.float32)  5.94 us
    dot_general x1, matrix products, one_tile(): jnp.einsum('gjrk,kgd->rgjd', weights, value_three, preferred_element_type...  3.37 us
    reduce_sum x1, other arithmetic, project(): jnp.mean(widened * widened, axis=1, keepdims=True) + EPS  3.23 us
  transfers between devices with their start and end apart: 10, of which 4 were waited for; matrix products, arithmetic and copies ran while one was open for 14% of the time, Pallas kernels for 0%

commit v1 on v0

--- a/solution.py
+++ b/solution.py
@@ -7,6 +7,11 @@
 DOC_MAX = 256
 EPS = 1e-05
 ROPE_BASE = 500000.0
+
+
+def tiled_gather(shard, axis, dim):
+    copies = jnp.concatenate([shard] * lax.axis_size(axis), axis=dim)
+    return lax.all_to_all(copies, axis, dim, dim, tiled=True)
 
 
 def from_behind(array, axis, by):
@@ -88,7 +93,7 @@
 
 
 def shards(hidden, norm_gain, w_query, w_key, w_value, doc_start, block_owner):
-    home_hidden = lax.all_gather(hidden, "tp", axis=0, tiled=True)
+    home_hidden = tiled_gather(hidden, "tp", 0)
     my_index = lax.axis_index("seq")
     home_rows = home_hidden.shape[0]
     home_blocks = block_owner.shape[0]

time: 143 us -> 133 us (0.930)
  between operations: 14.4 us -> 1 us
  waiting for transfers between devices: 46.3 us -> 34.4 us
  other arithmetic: 12.5 us -> 20.5 us
  local copies, waits for them, and re-layouts: 9.14 us -> 14.1 us
  starting transfers between devices: 29.3 us -> 34.2 us
    all_gather x1 -> x0, waiting for transfers between devices: 36.2 us -> none  [shards(): home_hidden = lax.all_gather(hidden, 'tp', axis=0, tiled=True)]
    all_to_all x0 -> x1, waiting for transfers between devices: none -> 28.4 us  [tiled_gather(): return lax.all_to_all(copies, axis, dim, dim, tiled=True)]
    dot_general x0 -> x2, local copies, waits for them, and re-layouts: none -> 10.5 us  [the longest x1 6.39 us: project(): queries = jnp.dot(normed, w_query, preferred_element_type=jnp.float32)]
    convert_element_type x0 -> x2, other arithmetic: none -> 7.79 us  [project(): normed = (widened * inverse_rms * norm_gain[None, :]).astype(jnp.bfloat16)]
    all_to_all x0 -> x1, starting transfers between devices: none -> 4.98 us  [tiled_gather(): return lax.all_to_all(copies, axis, dim, dim, tiled=True)]
    concatenate x0 -> x1, other arithmetic: none -> 4.24 us  [tiled_gather(): copies = jnp.concatenate([shard] * lax.axis_size(axis), axis=dim)]
    ppermute x9, waiting for transfers between devices: 9.44 us -> 5.98 us  [from_behind(): return lax.ppermute(array, axis, pairs)]
    another operation x2, other arithmetic: 1.76 us -> 0.27 us
  transfers between devices with their start and end apart: 10 -> 10, of which waited for: 4 -> 2; matrix products, arithmetic and copies ran while one was open for 14% -> 19% of each run, Pallas kernels for 0% -> 0%
where the time goes in v1:
time: 133 us
  waiting for transfers between devices  34.4 us (26%)
  starting transfers between devices  34.2 us (26%)
  other arithmetic  20.5 us (15%)
  matrix products  17.9 us (13%)
  local copies, waits for them, and re-layouts  14.1 us (11%)
  blocking collectives  10.5 us (8%)
    ppermute x9, starting transfers between devices, from_behind(): return lax.ppermute(array, axis, pairs)  29.3 us
    all_to_all x1, waiting for transfers between devices, tiled_gather(): return lax.all_to_all(copies, axis, dim, dim, tiled=True)  28.4 us
    all_to_all x1, blocking collectives, shards(): lax.all_to_all(home_context, 'tp', split_axis=0, concat_axis=1, tiled=True)  10.5 us
    convert_element_type x2, other arithmetic, project(): normed = (widened * inverse_rms * norm_gain[None, :]).astype(jnp.bfloat16)  7.79 us
    dot_general x1, local copies, waits for them, and re-layouts, project(): queries = jnp.dot(normed, w_query, preferred_element_type=jnp.float32)  6.39 us
    sub x1, matrix products, one_tile(): weights = jnp.exp(scores - highest)  6.17 us
    ppermute x9, waiting for transfers between devices, from_behind(): return lax.ppermute(array, axis, pairs)  5.98 us
    dot_general x1, matrix products, project(): queries = jnp.dot(normed, w_query, preferred_element_type=jnp.float32)  5.82 us
  transfers between devices with their start and end apart: 10, of which 2 were waited for; matrix products, arithmetic and copies ran while one was open for 19% of the time, Pallas kernels for 0%

profile of v1, /device:TPU:128, one launch (start us, length us, event | category | flops | bytes accessed | tf_op | source)
XLA Modules:
  0.0 132.6 jit_solution(14283194901348656739)
XLA Ops:
  0.6 4.2 %pad_maximum_fusion = bf16[512,4096]{1,0:T(8,128)(2,1)} fusion(bf16[128,4096]{1,0:T(8,128)(2,1)} %param.7), kind=kLoop, calls=%fused_computation.10 | loop fusion | flops 16777216 | bytes 5242880 | tf_op jit(solution)/shard_map/concatenate | solution.py:13
  4.9 5.0 %all-to-all-start = ((bf16[4,128,4096]{2,1,0:T(8,128)(2,1)}), bf16[4,128,4096]{2,1,0:T(8,128)(2,1)}, u32[]{:S(2)}, u32[]{:S(2)}) async-start(bf16[4,128,4096]{2,1,0:T(8,128)(2,1)} %bitcast.55), calls=%async_computation | async-start | bytes 8388608 | tf_op jit(solution)/shard_map/all_to_all | solution.py:14
  10.1 3.6 %collective-permute-start.4 = (s32[128]{0:T(128)S(1)}, s32[128]{0:T(128)S(1)}, u32[]{:S(2)}, u32[]{:S(2)}) collective-permute-start(s32[128]{0:T(128)S(1)} %slice.56), channel_id=1, source_target_pairs={{4,0},{8,4},{12,8},{16,12},{20,16},{24,20},{28,24},{32,28},{36,32}... | collective-permute-start | bytes 1544 | tf_op jit(solution)/shard_map/ppermute | solution.py:20
  13.9 1.9 %collective-permute-start.3 = (s32[128]{0:T(128)S(1)}, s32[128]{0:T(128)S(1)}, u32[]{:S(2)}, u32[]{:S(2)}) collective-permute-start(s32[128]{0:T(128)S(1)} %slice.54), channel_id=1, source_target_pairs={{0,4},{4,8},{8,12},{12,16},{16,20},{20,24},{24,28},{28,32},{32,36}... | collective-permute-start | bytes 1544 | tf_op jit(solution)/shard_map/ppermute | solution.py:20
  15.9 1.9 %collective-permute-start.1 = (s32[512]{0:T(512)S(1)}, s32[512]{0:T(512)S(1)}, u32[]{:S(2)}, u32[]{:S(2)}) collective-permute-start(s32[512]{0:T(512)S(1)} %copy-done.4), channel_id=1, source_target_pairs={{0,4},{4,8},{8,12},{12,16},{16,20},{20,24},{24,28},{28,32},{32,36}... | collective-permute-start | bytes 6152 | tf_op jit(solution)/shard_map/ppermute | solution.py:20
  18.6 4.1 %copy.36 = bf16[256,4096]{1,0:T(8,128)(2,1)} copy(bf16[256,4096]{0,1:T(8,128)(2,1)} %bitcast.60) | data formatting | bytes 4194304 | tf_op jit(solution)/shard_map/dot_general | solution.py:47
  22.7 6.4 %copy.40 = bf16[512,4096]{1,0:T(8,128)(2,1)} copy(bf16[512,4096]{0,1:T(8,128)(2,1)} %bitcast.58) | data formatting | bytes 8388608 | tf_op jit(solution)/shard_map/dot_general | solution.py:46
  29.1 1.5 %fusion.8 = pred[512,768]{0,1:T(8,128)(4,1)} fusion(s32[512]{0:T(512)S(1)} %iota_add_fusion.1, s32[512]{0:T(512)S(1)} %get-tuple-element.59, s32[512]{0:T(512)S(1)} %copy-done.4, s32[768]{0:T(1024)S(1)} %dynamic_slice.25, s32[768]{0:T(1024)S(1)} %dynamic_slice.24, pred[768]{0:T(1024)(128)(4,1)S(1)} %slice_compare_fusion), kind=kLoop, calls=%fused_computation.16 | loop fusion | flops 2359296 | bytes 406272 | tf_op jit(solution)/shard_map/while/body/eval_jaxpr/or | solution.py:81
  30.6 28.4 %all-to-all-done = bf16[4,128,4096]{2,1,0:T(8,128)(2,1)} async-done(((bf16[4,128,4096]{2,1,0:T(8,128)(2,1)}), bf16[4,128,4096]{2,1,0:T(8,128)(2,1)}, u32[]{:S(2)}, u32[]{:S(2)}) %all-to-all-start) | async-done | bytes 4194336 | tf_op jit(solution)/shard_map/all_to_all | solution.py:14
  59.0 3.1 %multiply_reduce_fusion = f32[4,128]{1,0:T(4,128)S(1)} fusion(bf16[4,128,4096]{2,1,0:T(8,128)(2,1)} %all-to-all-done), kind=kLoop, calls=%fused_computation.5 | loop fusion | flops 6290944 | bytes 4196352 | tf_op jit(solution)/shard_map/reduce_sum | solution.py:44
  62.1 3.8 %fusion.2 = bf16[512,4096]{1,0:T(8,128)(2,1)S(1)} fusion(bf16[4,128,4096]{2,1,0:T(8,128)(2,1)} %all-to-all-done, f32[4096]{0:T(1024)S(1)} %copy-done.3, f32[512]{0:T(512)S(1)} %get-tuple-element.51), kind=kLoop, calls=%fused_computation.3 | loop fusion | flops 8388608 | bytes 8407040 | tf_op jit(solution)/shard_map/convert_element_type | solution.py:45
  67.9 1.9 %collective-permute-start = (bf16[512,256]{1,0:T(8,128)(2,1)S(1)}, bf16[512,256]{1,0:T(8,128)(2,1)}, u32[]{:S(2)}, u32[]{:S(2)}) collective-permute-start(bf16[512,256]{1,0:T(8,128)(2,1)S(1)} %convolution_convert_fusion), channel_id=1, source_target_pairs={{0,4},{4,8},{8,12},{12,16},{16,20},{20,24},{24,28},{28,32},{32,36}... | collective-permute-start | bytes 786440 | tf_op jit(solution)/shard_map/ppermute | solution.py:20
  69.8 4.0 %multiply_convert_fusion = bf16[4,128,4096]{2,1,0:T(8,128)(2,1)S(1)} fusion(bf16[4,128,4096]{2,1,0:T(8,128)(2,1)} %all-to-all-done, f32[4096]{0:T(1024)S(1)} %copy-done.3, f32[4,128]{1,0:T(4,128)S(1)} %get-tuple-element.50), kind=kLoop, calls=%fused_computation.4 | loop fusion | flops 8388608 | bytes 8407040 | tf_op jit(solution)/shard_map/convert_element_type | solution.py:45
  75.8 7.0 %collective-permute-start.8 = (bf16[128,256]{1,0:T(8,128)(2,1)}, bf16[128,256]{1,0:T(8,128)(2,1)}, u32[]{:S(2)}, u32[]{:S(2)}) collective-permute-start(bf16[128,256]{1,0:T(8,128)(2,1)} %get-tuple-element.43), channel_id=1, source_target_pairs={{4,0},{8,4},{12,8},{16,12},{20,16},{24,20},{28,24},{32,28},{36,32}... | collective-permute-start | bytes 196616 | tf_op jit(solution)/shard_map/ppermute | solution.py:20
  82.8 1.9 %collective-permute-start.7 = (bf16[128,256]{1,0:T(8,128)(2,1)}, bf16[128,256]{1,0:T(8,128)(2,1)}, u32[]{:S(2)}, u32[]{:S(2)}) collective-permute-start(bf16[128,256]{1,0:T(8,128)(2,1)} %get-tuple-element.42), channel_id=1, source_target_pairs={{0,4},{4,8},{8,12},{12,16},{16,20},{20,24},{24,28},{28,32},{32,36}... | collective-permute-start | bytes 196616 | tf_op jit(solution)/shard_map/ppermute | solution.py:20
  84.9 1.9 %collective-permute-start.2 = (bf16[512,256]{1,0:T(8,128)(2,1)S(1)}, bf16[512,256]{1,0:T(8,128)(2,1)}, u32[]{:S(2)}, u32[]{:S(2)}) collective-permute-start(bf16[512,256]{1,0:T(8,128)(2,1)S(1)} %copy.37), channel_id=1, source_target_pairs={{0,4},{4,8},{8,12},{12,16},{16,20},{20,24},{24,28},{28,32},{32,36}... | collective-permute-start | bytes 786440 | tf_op jit(solution)/shard_map/ppermute | solution.py:20
  86.9 7.0 %collective-permute-start.6 = (bf16[128,256]{1,0:T(8,128)(2,1)S(1)}, bf16[128,256]{1,0:T(8,128)(2,1)}, u32[]{:S(2)}, u32[]{:S(2)}) collective-permute-start(bf16[128,256]{1,0:T(8,128)(2,1)S(1)} %copy.42), channel_id=1, source_target_pairs={{4,0},{8,4},{12,8},{16,12},{20,16},{24,20},{28,24},{32,28},{36,32}... | collective-permute-start | bytes 196616 | tf_op jit(solution)/shard_map/ppermute | solution.py:20
  93.9 5.8 %fusion.38 = f32[512,4,128]{0,2,1:T(8,128)S(1)} fusion(bf16[512,4096,1]{1,0,2:T(8,128)(2,1)} %bitcast.57, bf16[4,128,4096]{2,1,0:T(8,128)(2,1)} %bitcast.59), kind=kOutput, calls=%fused_computation.65 | convolution fusion | flops 2147483648 | bytes 9437184 | tf_op jit(solution)/shard_map/dot_general | solution.py:46
  100.0 2.1 %collective-permute-start.5 = (bf16[128,256]{1,0:T(8,128)(2,1)S(1)}, bf16[128,256]{1,0:T(8,128)(2,1)S(1)}, u32[]{:S(2)}, u32[]{:S(2)}) collective-permute-start(bf16[128,256]{1,0:T(8,128)(2,1)S(1)} %copy.41), channel_id=1, source_target_pairs={{0,4},{4,8},{8,12},{12,16},{16,20},{20,24},{24,28},{28,32},{32,36}... | collective-permute-start | bytes 196616 | tf_op jit(solution)/shard_map/ppermute | solution.py:20
  103.0 6.0 %collective-permute-done.5 = bf16[128,256]{1,0:T(8,128)(2,1)S(1)} collective-permute-done((bf16[128,256]{1,0:T(8,128)(2,1)S(1)}, bf16[128,256]{1,0:T(8,128)(2,1)S(1)}, u32[]{:S(2)}, u32[]{:S(2)}) %collective-permute-start.5) | collective-permute-done | bytes 65568 | tf_op jit(solution)/shard_map/ppermute | solution.py:20
  108.9 2.2 %maximum_select_fusion.1 = (bf16[768,256]{1,0:T(8,128)(2,1)}, bf16[768,256]{1,0:T(8,128)(2,1)S(1)}, bf16[768,256]{1,0:T(8,128)(2,1)S(1)}, bf16[768,256]{1,0:T(8,128)(2,1)}) fusion(bf16[128,256]{1,0:T(8,128)(2,1)} %collective-permute-done.8, bf16[512,256]{1,0:T(8,128)(2,1)S(1)} %convolution_convert_fusion, bf16[128,256]{1,0:T(8,128)(2,1)} %collective-permute-done.7, ...), kind=kLoop, calls=%fused_computation.27 | loop fusion | flops 4325376 | bytes 2884352 | tf_op jit(solution)/shard_map/jit(_where)/select_n | solution.py:142
  111.4 6.2 %fusion.32 = (f32[2,2,512]{2,1,0:T(2,128)S(1)}, f32[2,2,512,768]{2,3,1,0:T(8,128)}) fusion(pred[512,768]{0,1:T(8,128)(4,1)} %fusion.8, bf16[512,2,2,128]{0,3,2,1:T(8,128)(2,1)} %bitcast.64, bf16[768,2,128,1]{2,1,0,3:T(2,128)(2,1)S(1)} %bitcast.66), kind=kOutput, calls=%fused_computation.63 | convolution fusion | flops 408945408 | bytes 7610368 | tf_op jit(solution)/shard_map/while/body/eval_jaxpr/sub | solution.py:84
  117.5 3.4 %fusion.10 = bf16[512,2,2,128]{0,3,2,1:T(8,128)(2,1)S(1)} fusion(bf16[768,2,128,1]{0,2,3,1:T(8,128)(2,1)S(1)} %bitcast.65, f32[2,2,512,768]{2,3,1,0:T(8,128)} %get-tuple-element.57, f32[2,2,512]{2,1,0:T(2,128)S(1)} %get-tuple-element.56), kind=kOutput, calls=%fused_computation.18 | convolution fusion | flops 406061056 | bytes 7217152 | tf_op jit(solution)/shard_map/while/body/eval_jaxpr/gjrk,kgd->rgjd/dot_general | solution.py:86
  121.1 10.5 %all_to_all.28 = bf16[4,128,512]{1,2,0:T(8,128)(2,1)S(1)} all-to-all(bf16[4,128,512]{1,2,0:T(8,128)(2,1)S(1)} %copy.27), channel_id=1, replica_groups=mesh['seq'=64,'tp'=4] {'tp'}, dimensions={0} | all-to-all | bytes 1048576 | tf_op jit(solution)/shard_map/all_to_all | solution.py:143
  (56 shorter events, 7.9 us)
Async XLA Ops:
  0.6 65.3 %copy-start = (bf16[4096,256]{1,0:T(8,128)(2,1)S(1)}, bf16[4096,256]{1,0:T(8,128)(2,1)}, u32[]{:S(2)}) copy-start(bf16[4096,256]{1,0:T(8,128)(2,1)} %param.11) | copy-start | bytes 6291460
  4.9 5.0 %copy-start.5 = (s32[16]{0:T(128)S(1)}, s32[16]{0:T(128)}, u32[]{:S(2)}) copy-start(s32[16]{0:T(128)} %param.13) | copy-start | bytes 196
  4.9 11.0 %copy-start.4 = (s32[512]{0:T(512)S(1)}, s32[512]{0:T(512)}, u32[]{:S(2)}) copy-start(s32[512]{0:T(512)} %param.12) | copy-start | bytes 6148
  4.9 54.1 %all-to-all-start = ((bf16[4,128,4096]{2,1,0:T(8,128)(2,1)}), bf16[4,128,4096]{2,1,0:T(8,128)(2,1)}, u32[]{:S(2)}, u32[]{:S(2)}) async-start(bf16[4,128,4096]{2,1,0:T(8,128)(2,1)} %bitcast.55), calls=%async_computation | async-start | bytes 8388608 | tf_op jit(solution)/shard_map/all_to_all | solution.py:14
  10.1 19.0 %collective-permute-start.4 = (s32[128]{0:T(128)S(1)}, s32[128]{0:T(128)S(1)}, u32[]{:S(2)}, u32[]{:S(2)}) collective-permute-start(s32[128]{0:T(128)S(1)} %slice.56), channel_id=1, source_target_pairs={{4,0},{8,4},{12,8},{16,12},{20,16},{24,20},{28,24},{32,28},{36,32}... | collective-permute-start | bytes 1544 | tf_op jit(solution)/shard_map/ppermute | solution.py:20
  13.9 15.2 %collective-permute-start.3 = (s32[128]{0:T(128)S(1)}, s32[128]{0:T(128)S(1)}, u32[]{:S(2)}, u32[]{:S(2)}) collective-permute-start(s32[128]{0:T(128)S(1)} %slice.54), channel_id=1, source_target_pairs={{0,4},{4,8},{8,12},{12,16},{16,20},{20,24},{24,28},{28,32},{32,36}... | collective-permute-start | bytes 1544 | tf_op jit(solution)/shard_map/ppermute | solution.py:20
  15.9 13.3 %collective-permute-start.1 = (s32[512]{0:T(512)S(1)}, s32[512]{0:T(512)S(1)}, u32[]{:S(2)}, u32[]{:S(2)}) collective-permute-start(s32[512]{0:T(512)S(1)} %copy-done.4), channel_id=1, source_target_pairs={{0,4},{4,8},{8,12},{12,16},{16,20},{20,24},{24,28},{28,32},{32,36}... | collective-permute-start | bytes 6152 | tf_op jit(solution)/shard_map/ppermute | solution.py:20
  29.1 33.0 %copy-start.3 = (f32[4096]{0:T(1024)S(1)}, f32[4096]{0:T(1024)}, u32[]{:S(2)}) copy-start(f32[4096]{0:T(1024)} %param.8) | copy-start | bytes 49156
  67.9 41.0 %collective-permute-start = (bf16[512,256]{1,0:T(8,128)(2,1)S(1)}, bf16[512,256]{1,0:T(8,128)(2,1)}, u32[]{:S(2)}, u32[]{:S(2)}) collective-permute-start(bf16[512,256]{1,0:T(8,128)(2,1)S(1)} %convolution_convert_fusion), channel_id=1, source_target_pairs={{0,4},{4,8},{8,12},{12,16},{16,20},{20,24},{24,28},{28,32},{32,36}... | collective-permute-start | bytes 786440 | tf_op jit(solution)/shard_map/ppermute | solution.py:20
  69.8 4.0 %copy-start.2 = (bf16[256,4096]{1,0:T(8,128)(2,1)S(1)}, bf16[256,4096]{1,0:T(8,128)(2,1)}, u32[]{:S(2)}) copy-start(bf16[256,4096]{1,0:T(8,128)(2,1)} %copy.36) | copy-start | bytes 6291460
  73.8 2.0 %copy-start.1 = (bf16[4,128,4096]{2,1,0:T(8,128)(2,1)}, bf16[4,128,4096]{2,1,0:T(8,128)(2,1)S(1)}, u32[]{:S(2)}) copy-start(bf16[4,128,4096]{2,1,0:T(8,128)(2,1)S(1)} %multiply_convert_fusion) | copy-start | bytes 12582916
  75.8 24.2 %collective-permute-start.8 = (bf16[128,256]{1,0:T(8,128)(2,1)}, bf16[128,256]{1,0:T(8,128)(2,1)}, u32[]{:S(2)}, u32[]{:S(2)}) collective-permute-start(bf16[128,256]{1,0:T(8,128)(2,1)} %get-tuple-element.43), channel_id=1, source_target_pairs={{4,0},{8,4},{12,8},{16,12},{20,16},{24,20},{28,24},{32,28},{36,32}... | collective-permute-start | bytes 196616 | tf_op jit(solution)/shard_map/ppermute | solution.py:20
  82.8 20.2 %collective-permute-start.7 = (bf16[128,256]{1,0:T(8,128)(2,1)}, bf16[128,256]{1,0:T(8,128)(2,1)}, u32[]{:S(2)}, u32[]{:S(2)}) collective-permute-start(bf16[128,256]{1,0:T(8,128)(2,1)} %get-tuple-element.42), channel_id=1, source_target_pairs={{0,4},{4,8},{8,12},{12,16},{16,20},{20,24},{24,28},{28,32},{32,36}... | collective-permute-start | bytes 196616 | tf_op jit(solution)/shard_map/ppermute | solution.py:20
  84.9 24.1 %collective-permute-start.2 = (bf16[512,256]{1,0:T(8,128)(2,1)S(1)}, bf16[512,256]{1,0:T(8,128)(2,1)}, u32[]{:S(2)}, u32[]{:S(2)}) collective-permute-start(bf16[512,256]{1,0:T(8,128)(2,1)S(1)} %copy.37), channel_id=1, source_target_pairs={{0,4},{4,8},{8,12},{12,16},{16,20},{20,24},{24,28},{28,32},{32,36}... | collective-permute-start | bytes 786440 | tf_op jit(solution)/shard_map/ppermute | solution.py:20
  86.9 16.1 %collective-permute-start.6 = (bf16[128,256]{1,0:T(8,128)(2,1)S(1)}, bf16[128,256]{1,0:T(8,128)(2,1)}, u32[]{:S(2)}, u32[]{:S(2)}) collective-permute-start(bf16[128,256]{1,0:T(8,128)(2,1)S(1)} %copy.42), channel_id=1, source_target_pairs={{4,0},{8,4},{12,8},{16,12},{20,16},{24,20},{28,24},{32,28},{36,32}... | collective-permute-start | bytes 196616 | tf_op jit(solution)/shard_map/ppermute | solution.py:20
  100.0 8.9 %collective-permute-start.5 = (bf16[128,256]{1,0:T(8,128)(2,1)S(1)}, bf16[128,256]{1,0:T(8,128)(2,1)S(1)}, u32[]{:S(2)}, u32[]{:S(2)}) collective-permute-start(bf16[128,256]{1,0:T(8,128)(2,1)S(1)} %copy.41), channel_id=1, source_target_pairs={{0,4},{4,8},{8,12},{12,16},{16,20},{20,24},{24,28},{28,32},{32,36}... | collective-permute-start | bytes 196616 | tf_op jit(solution)/shard_map/ppermute | solution.py:20
